TPU v7x, 32 devices: a whole 2x2x4 slice. The times are simulated.
32 devices in a mesh: seq: 16 (over z, x, core), group: 2 (over y).
Axes of the slice: x: 2, y: 2, z: 4, core: 2. Of those that a mesh axis runs over, the one named last changes fastest.
Arguments:
- prefix_keys: bfloat16 [4096, 512], P(('group', 'seq')), parts along dimension 0, may hold values from -5 to 5
- prefix_values: bfloat16 [4096, 512], P(('group', 'seq')), parts along dimension 0, may hold values from -6 to 6
- round_queries: bfloat16 [2048, 2048], P(('group', 'seq')), parts along dimension 0, may hold values from -5 to 5
- round_keys: bfloat16 [2048, 512], P(('group', 'seq')), parts along dimension 0, may hold values from -5 to 5
- round_values: bfloat16 [2048, 512], P(('group', 'seq')), parts along dimension 0, may hold values from -6 to 6
- d_out: bfloat16 [2048, 2048], P(('group', 'seq')), parts along dimension 0, may hold values from -6 to 6
- prefix_agent: int32 [4096], P('group'), parts along dimension 0, may hold values from 0 to 7
- prefix_round: int32 [4096], P('group'), parts along dimension 0, may hold values from 0 to 15, never falling along the last dimension, each value on 1 to 256 neighbouring positions
- round_agent: int32 [2048], P('group'), parts along dimension 0, may hold values from 0 to 7
Outputs:
- attn_out: bfloat16 [2048, 2048], P(('group', 'seq')), parts along dimension 0
- d_round_queries: bfloat16 [2048, 2048], P(('group', 'seq')), parts along dimension 0
- d_round_keys: bfloat16 [2048, 512], P(('group', 'seq')), parts along dimension 0
- d_round_values: bfloat16 [2048, 512], P(('group', 'seq')), parts along dimension 0
- d_prefix_keys: bfloat16 [4096, 512], P(('group', 'seq')), parts along dimension 0
- d_prefix_values: bfloat16 [4096, 512], P(('group', 'seq')), parts along dimension 0
There are 2 independent parts, one for each index of `group`. A program takes and returns all parts, laid end to end along the dimension named above; each array names one. Nothing has to cross between parts.
Inputs may be any that keep to these rules, and one draw needn't show every extreme that they name: `prefix_round`: never falls along positions; every round has at least one token.
All inputs are finite; a program needn't handle non-finite values.
Results may differ from a plain program's by a relative error of at most 0.017.
Values may be sent and summed in bfloat16 or wider, within the bound.
A program may use at most 128 MiB of HBM per device.

v0:
```python
import math

import jax
import jax.numpy as jnp
from jax import lax
from jax.sharding import PartitionSpec as P

HQ = 16
KVH = 4
DH = 128
ROUNDS = 16


def to_head_rows(local, devices):
    splits = devices // HQ
    quarter_rows = local.shape[0] // splits
    shaped = local.reshape(splits, quarter_rows, HQ, DH).transpose(2, 0, 1, 3)
    return shaped.reshape(devices, quarter_rows, DH)


def from_head_rows(received, devices):
    splits = devices // HQ
    quarter_rows = received.shape[1]
    shaped = received.reshape(HQ, splits, quarter_rows, DH).transpose(1, 2, 0, 3)
    return shaped.reshape(splits * quarter_rows, HQ * DH)


def spread_heads(local, devices):
    local_keys = local.shape[0]
    shaped = local.reshape(local_keys, KVH, DH).transpose(1, 0, 2)
    shaped = jnp.broadcast_to(shaped[:, None], (KVH, devices // KVH, local_keys, DH))
    return shaped.reshape(devices, local_keys, DH)


def sum_groups(received, devices):
    local_keys = received.shape[1]
    summed = received.reshape(KVH, devices // KVH, local_keys, DH).sum(1)
    return summed.transpose(1, 0, 2).reshape(local_keys, KVH * DH)


def body(
    prefix_keys,
    prefix_values,
    round_queries,
    round_keys,
    round_values,
    d_out,
    prefix_agent,
    prefix_round,
    round_agent,
):
    devices = lax.axis_size("seq")
    device_index = lax.axis_index("seq")
    splits = devices // HQ
    own_rows = round_queries.shape[0]
    quarter_rows = own_rows // splits
    pre_rows = prefix_keys.shape[0]
    local_keys = pre_rows + own_rows
    score_scale = DH ** (-0.5)
    own_block = device_index % splits
    keys_local = jnp.concatenate([prefix_keys, round_keys], 0)
    values_local = jnp.concatenate([prefix_values, round_values], 0)
    query_head, grad_head = (
        lax.all_to_all(
            to_head_rows(round_queries, devices), "seq", split_axis=0, concat_axis=0, tiled=True
        ),
        lax.all_to_all(
            to_head_rows(d_out, devices), "seq", split_axis=0, concat_axis=0, tiled=True
        ),
    )
    query_head = query_head.reshape(devices * quarter_rows, DH)
    grad_head = grad_head.reshape(devices * quarter_rows, DH)
    head_rows = devices * quarter_rows
    key_head, value_head = (
        lax.all_to_all(
            spread_heads(keys_local, devices), "seq", split_axis=0, concat_axis=0, tiled=True
        ),
        lax.all_to_all(
            spread_heads(values_local, devices), "seq", split_axis=0, concat_axis=0, tiled=True
        ),
    )
    source = jnp.arange(devices, dtype=jnp.int32)
    query_pos = (
        source[:, None] * own_rows
        + own_block * quarter_rows
        + jnp.arange(quarter_rows, dtype=jnp.int32)[None, :]
    ).reshape(-1)
    query_agent = round_agent[query_pos]
    key_slot = jnp.arange(local_keys, dtype=jnp.int32)
    pre_index = source[:, None] * pre_rows + jnp.minimum(key_slot, pre_rows - 1)[None, :]
    round_index = source[:, None] * own_rows + jnp.maximum(key_slot - pre_rows, 0)[None, :]
    key_agent = prefix_agent[pre_index]
    key_public = prefix_round[pre_index] < ROUNDS - 2
    key_prefix = jnp.broadcast_to((key_slot < pre_rows)[None, :], (devices, local_keys))
    block_shards = math.gcd(devices, 16)
    blocks = devices // block_shards
    block_keys = block_shards * local_keys
    key_blocks = key_head.reshape(blocks, block_keys, DH)
    value_blocks = value_head.reshape(blocks, block_keys, DH)
    key_info = (
        key_agent.reshape(blocks, block_keys),
        key_public.reshape(blocks, block_keys),
        key_prefix.reshape(blocks, block_keys),
        round_index.reshape(blocks, block_keys),
    )

    def block_scores(key_blk, info):
        agent_b, public_b, prefix_b, order_b = info
        visible = jnp.where(
            prefix_b[None, :],
            public_b[None, :] | (agent_b[None, :] == query_agent[:, None]),
            order_b[None, :] <= query_pos[:, None],
        )
        raw = (
            jnp.einsum("qd,kd->qk", query_head, key_blk, preferred_element_type=jnp.float32)
            * score_scale
        )
        return jnp.where(visible, raw, -jnp.inf)

    def stat_step(carry, blk):
        top, total = carry
        masked = block_scores(blk[0], blk[1])
        new_top = jnp.maximum(top, jnp.max(masked, 1, keepdims=True))
        total = total * jnp.exp(top - new_top) + jnp.sum(
            jnp.exp(masked - new_top), 1, keepdims=True
        )
        return ((new_top, total), None)

    start_stats = (
        jnp.full((head_rows, 1), -1e30, jnp.float32),
        jnp.zeros((head_rows, 1), jnp.float32),
    )
    (top_score, total_exp), _ = lax.scan(stat_step, start_stats, (key_blocks, key_info))
    log_total = top_score + jnp.log(total_exp)

    def out_step(acc, blk):
        masked = block_scores(blk[0], blk[2])
        probs_low = jnp.exp(masked - log_total).astype(jnp.bfloat16)
        return (acc + jnp.dot(probs_low, blk[1], preferred_element_type=jnp.float32), None)

    out_acc, _ = lax.scan(
        out_step, jnp.zeros((head_rows, DH), jnp.float32), (key_blocks, value_blocks, key_info)
    )
    attended = out_acc.astype(jnp.bfloat16)
    attn_rows = lax.all_to_all(
        attended.reshape(devices, quarter_rows, DH), "seq", split_axis=0, concat_axis=0, tiled=True
    )
    attn_out = from_head_rows(attn_rows, devices)
    delta = jnp.sum(grad_head.astype(jnp.float32) * attended.astype(jnp.float32), 1, keepdims=True)

    def back_step(acc, blk):
        key_blk, value_blk, info = blk
        masked = block_scores(key_blk, info)
        probs = jnp.exp(masked - log_total)
        grad_probs = jnp.einsum(
            "qd,kd->qk", grad_head, value_blk, preferred_element_type=jnp.float32
        )
        grad_scores = (probs * (grad_probs - delta) * score_scale).astype(jnp.bfloat16)
        acc = acc + jnp.dot(grad_scores, key_blk, preferred_element_type=jnp.float32)
        key_part = jnp.einsum(
            "qk,qd->kd", grad_scores, query_head, preferred_element_type=jnp.float32
        )
        value_part = jnp.einsum(
            "qk,qd->kd", probs.astype(jnp.bfloat16), grad_head, preferred_element_type=jnp.float32
        )
        return (acc, (key_part, value_part))

    start_grad = jnp.zeros((head_rows, DH), jnp.float32)
    query_acc, parts = lax.scan(
        lambda acc, blk: back_step(acc, blk), start_grad, (key_blocks, value_blocks, key_info)
    )
    key_part = parts[0].reshape(devices, local_keys, DH)
    value_part = parts[1].reshape(devices, local_keys, DH)
    key_sum, value_sum = (
        lax.all_to_all(key_part, "seq", split_axis=0, concat_axis=0, tiled=True),
        lax.all_to_all(value_part, "seq", split_axis=0, concat_axis=0, tiled=True),
    )
    grad_keys = sum_groups(key_sum, devices)
    grad_values = sum_groups(value_sum, devices)
    grad_query = query_acc.astype(jnp.bfloat16)
    query_rows = lax.all_to_all(
        grad_query.reshape(devices, quarter_rows, DH),
        "seq",
        split_axis=0,
        concat_axis=0,
        tiled=True,
    )
    d_round_queries = from_head_rows(query_rows, devices)
    keys_low = grad_keys.astype(jnp.bfloat16)
    values_low = grad_values.astype(jnp.bfloat16)
    return (
        attn_out,
        d_round_queries,
        keys_low[pre_rows:],
        values_low[pre_rows:],
        keys_low[:pre_rows],
        values_low[:pre_rows],
    )


def solution(mesh):
    placed = (
        P(("group", "seq"), None),
        P(("group", "seq"), None),
        P(("group", "seq"), None),
        P(("group", "seq"), None),
        P(("group", "seq"), None),
        P(("group", "seq"), None),
        P("group"),
        P("group"),
        P("group"),
    )
    return jax.shard_map(
        body,
        mesh=mesh,
        in_specs=placed,
        out_specs=(
            P(("group", "seq"), None),
            P(("group", "seq"), None),
            P(("group", "seq"), None),
            P(("group", "seq"), None),
            P(("group", "seq"), None),
            P(("group", "seq"), None),
        ),
        check_vma=False,
    )
```

profile of v0, /device:TPU:0, one launch (start us, length us, event | category | flops | bytes accessed | tf_op | source)
XLA Modules:
  0.0 239.8 jit_solution(6571877653069009306)
XLA Ops:
  0.7 1.0 copy.47
  2.4 7.4 %all-to-all-start.1 = ((bf16[16,64,128]{2,1,0:T(8,128)(2,1)}), bf16[16,64,128]{2,1,0:T(8,128)(2,1)S(1)}, u32[]{:S(2)}, u32[]{:S(2)}) async-start(bf16[16,64,128]{2,1,0:T(8,128)(2,1)} %bitcast.93), calls=%async_computation.1 | async-start | bytes 524288 | tf_op jit(solution)/shard_map/all_to_all | solution.py:64
  9.8 1.0 copy.49
  11.6 1.0 pad_maximum_fusion
  12.5 7.3 %all-to-all-done.1 = bf16[16,64,128]{2,1,0:T(8,128)(2,1)S(1)} async-done(((bf16[16,64,128]{2,1,0:T(8,128)(2,1)}), bf16[16,64,128]{2,1,0:T(8,128)(2,1)S(1)}, u32[]{:S(2)}, u32[]{:S(2)}) %all-to-all-start.1) | async-done | bytes 262176 | tf_op jit(solution)/shard_map/all_to_all | solution.py:64
  19.8 3.5 %all-to-all-start.4 = ((bf16[16,64,128]{2,1,0:T(8,128)(2,1)}), bf16[16,64,128]{2,1,0:T(8,128)(2,1)S(1)}, u32[]{:S(2)}, u32[]{:S(2)}) async-start(bf16[16,64,128]{2,1,0:T(8,128)(2,1)} %bitcast.92), calls=%async_computation.4 | async-start | bytes 524288 | tf_op jit(solution)/shard_map/all_to_all | solution.py:67
  23.6 9.8 %all-to-all-done.4 = bf16[16,64,128]{2,1,0:T(8,128)(2,1)S(1)} async-done(((bf16[16,64,128]{2,1,0:T(8,128)(2,1)}), bf16[16,64,128]{2,1,0:T(8,128)(2,1)S(1)}, u32[]{:S(2)}, u32[]{:S(2)}) %all-to-all-start.4) | async-done | bytes 262176 | tf_op jit(solution)/shard_map/all_to_all | solution.py:67
  33.4 1.1 broadcast_in_dim.106
  34.5 3.6 %all-to-all-start = ((bf16[16,192,128]{2,1,0:T(8,128)(2,1)}), bf16[16,192,128]{2,1,0:T(8,128)(2,1)S(1)}, u32[]{:S(2)}, u32[]{:S(2)}) async-start(bf16[16,192,128]{2,1,0:T(8,128)(2,1)} %bitcast.2), calls=%async_computation | async-start | bytes 1572864 | tf_op jit(solution)/shard_map/all_to_all | solution.py:75
  38.6 17.4 %gather_fusion.1 = s32[3072]{0:T(1024)S(1)} fusion(s32[2048]{0:T(1024)S(1)} %copy-done, s32[3072]{0:T(1024)S(1)} %broadcast_clamp_fusion), kind=kCustom, calls=%fused_computation.1 | custom fusion | bytes 36864 | tf_op jit(solution)/shard_map/gather | solution.py:92
  56.1 17.4 %gather_fusion = s32[3072]{0:T(1024)S(1)} fusion(s32[2048]{0:T(1024)S(1)} %copy-done.1, s32[3072]{0:T(1024)S(1)} %broadcast_clamp_fusion), kind=kCustom, calls=%fused_computation | custom fusion | bytes 36864 | tf_op jit(solution)/shard_map/gather | solution.py:93
  73.6 4.5 %gather_fusion.2 = s32[1024]{0:T(1024)S(1)} fusion(s32[1024]{0:T(1024)S(1)} %copy-done.2, s32[1024]{0:T(1024)S(1)} %broadcast_clamp_fusion.1), kind=kCustom, calls=%fused_computation.2 | custom fusion | bytes 12288 | tf_op jit(solution)/shard_map/gather | solution.py:88
  78.2 1.1 broadcast_in_dim.110
  79.3 6.0 %all-to-all-start.2 = ((bf16[16,192,128]{2,1,0:T(8,128)(2,1)}), bf16[16,192,128]{2,1,0:T(8,128)(2,1)S(1)}, u32[]{:S(2)}, u32[]{:S(2)}) async-start(bf16[16,192,128]{2,1,0:T(8,128)(2,1)} %bitcast.9), calls=%async_computation.2 | async-start | bytes 1572864 | tf_op jit(solution)/shard_map/all_to_all | solution.py:78
  85.3 10.2 %fusion.16 = (f32[1024]{0:T(1024)S(1)}, f32[1024,3072]{0,1:T(8,128)S(1)}, f32[3072,1024]{1,0:T(8,128)}) fusion(s32[1024]{0:T(1024)S(1)} %add.176, s32[3072]{0:T(1024)S(1)} %add.175, s32[1024]{0:T(1024)S(1)} %gather_fusion.2, s32[3072]{0:T(1024)S(1)} %gather_fusion.1, pred[3072]{0:T(1024)(128)(4,1)S(1)} %broadcast_compare_fusion, ...), kind=kOutput, calls=%fused_computation.48 | convolution fusion | flops 827325440 | bytes 26257408 | tf_op jit(solution)/shard_map/while/body/eval_jaxpr/qd,kd->qk/dot_general | solution.py:115
  95.5 4.5 %copy-done.3 = f32[1024,3072]{0,1:T(8,128)} copy-done((f32[1024,3072]{0,1:T(8,128)}, f32[1024,3072]{0,1:T(8,128)S(1)}, u32[]{:S(2)}) %copy-start.3) | copy-done | bytes 12582936
  99.9 1.7 exponential_reduce_fusion
  101.7 2.3 all-to-all-done.2
  104.0 7.2 %multiply_reduce_fusion = (f32[1024]{0:T(1024)S(1)}, bf16[1024,128]{1,0:T(8,128)(2,1)}) fusion(bf16[16,64,128]{2,1,0:T(8,128)(2,1)S(1)} %all-to-all-done.4, bf16[3072,128]{1,0:T(8,128)(2,1)S(1)} %bitcast.96, f32[1024,3072]{0,1:T(8,128)} %copy-done.3, f32[1024]{0:T(1024)S(1)} %log_add_fusion), kind=kOutput, calls=%fused_computation.20 | convolution fusion | flops 812252160 | bytes 13901824 | tf_op jit(solution)/shard_map/while/body/eval_jaxpr/dot_general | solution.py:139
  111.2 5.5 %all-to-all-start.3 = ((bf16[16,64,128]{2,1,0:T(8,128)(2,1)}), bf16[16,64,128]{2,1,0:T(8,128)(2,1)S(1)}, u32[]{:S(2)}, u32[]{:S(2)}) async-start(bf16[16,64,128]{2,1,0:T(8,128)(2,1)} %bitcast.11), calls=%async_computation.3 | async-start | bytes 524288 | tf_op jit(solution)/shard_map/all_to_all | solution.py:145
  116.7 18.6 %fusion.3 = (bf16[3072,1024]{1,0:T(8,128)(2,1)}, bf16[3072,1024]{1,0:T(8,128)(2,1)}, f32[3072,1024]{1,0:T(8,128)}) fusion(f32[3072,1024]{1,0:T(8,128)} %get-tuple-element.101, f32[1024]{0:T(1024)S(1)} %log_add_fusion, s32[1024]{0:T(1024)S(1)} %add.176, s32[1024]{0:T(1024)S(1)} %gather_fusion.2, s32[3072]{0:T(1024)S(1)} %add.175, ...), kind=kOutput, calls=%fused_computation.12 | convolution fusion | flops 843055104 | bytes 38844416 | tf_op jit(solution)/shard_map/while/body/eval_jaxpr/qd,kd->qk/dot_general | solution.py:155
  135.3 9.1 %fusion.9 = bf16[1024,128]{1,0:T(8,128)(2,1)} fusion(bf16[3072,128]{1,0:T(8,128)(2,1)S(1)} %bitcast.99, f32[3072,1024]{1,0:T(8,128)} %get-tuple-element.104, f32[1024,3072]{0,1:T(8,128)S(1)} %copy-done.4, f32[1024]{0:T(1024)S(1)} %get-tuple-element.102, f32[1024]{0:T(1024)S(1)} %log_add_fusion), kind=kOutput, calls=%fused_computation.18 | convolution fusion | flops 821166080 | bytes 26222592 | tf_op jit(solution)/shard_map/while/body/eval_jaxpr/dot_general | solution.py:159
  144.4 6.0 %all-to-all-start.5 = ((bf16[16,64,128]{2,1,0:T(8,128)(2,1)}), bf16[16,64,128]{2,1,0:T(8,128)(2,1)S(1)}, u32[]{:S(2)}, u32[]{:S(2)}) async-start(bf16[16,64,128]{2,1,0:T(8,128)(2,1)} %bitcast.18), calls=%async_computation.5 | async-start | bytes 524288 | tf_op jit(solution)/shard_map/all_to_all | solution.py:181
  150.4 5.8 %fusion.18 = f32[16,192,128]{2,1,0:T(8,128)} fusion(bf16[16,192,1024]{2,1,0:T(8,128)(2,1)} %bitcast.95, bf16[1024,128,1]{1,0,2:T(8,128)(2,1)S(1)} %bitcast.101), kind=kOutput, calls=%fused_computation.50 | convolution fusion | flops 805306368 | bytes 8126464 | tf_op jit(solution)/shard_map/while/body/eval_jaxpr/qk,qd->kd/dot_general | solution.py:163
  156.2 4.3 %all-to-all-done.5 = bf16[16,64,128]{2,1,0:T(8,128)(2,1)S(1)} async-done(((bf16[16,64,128]{2,1,0:T(8,128)(2,1)}), bf16[16,64,128]{2,1,0:T(8,128)(2,1)S(1)}, u32[]{:S(2)}, u32[]{:S(2)}) %all-to-all-start.5) | async-done | bytes 262176 | tf_op jit(solution)/shard_map/all_to_all | solution.py:181
  160.5 3.7 %all-to-all-start.7 = ((f32[16,192,128]{2,1,0:T(8,128)}), f32[16,192,128]{2,1,0:T(8,128)S(1)}, u32[]{:S(2)}, u32[]{:S(2)}) async-start(f32[16,192,128]{2,1,0:T(8,128)} %fusion.18), calls=%async_computation.7 | async-start | bytes 3145728 | tf_op jit(solution)/shard_map/all_to_all | solution.py:176
  164.2 5.7 %fusion.17 = f32[16,192,128]{2,1,0:T(8,128)} fusion(bf16[16,192,1024]{2,1,0:T(8,128)(2,1)} %bitcast.94, bf16[1024,128,1]{1,0,2:T(8,128)(2,1)S(1)} %bitcast.103), kind=kOutput, calls=%fused_computation.49 | convolution fusion | flops 805306368 | bytes 8126464 | tf_op jit(solution)/shard_map/while/body/eval_jaxpr/qk,qd->kd/dot_general | solution.py:160
  169.9 26.2 %all-to-all-done.7 = f32[16,192,128]{2,1,0:T(8,128)S(1)} async-done(((f32[16,192,128]{2,1,0:T(8,128)}), f32[16,192,128]{2,1,0:T(8,128)S(1)}, u32[]{:S(2)}, u32[]{:S(2)}) %all-to-all-start.7) | async-done | bytes 1572896 | tf_op jit(solution)/shard_map/all_to_all | solution.py:176
  196.1 9.1 %all-to-all-start.6 = ((f32[16,192,128]{2,1,0:T(8,128)}), f32[16,192,128]{2,1,0:T(8,128)S(1)}, u32[]{:S(2)}, u32[]{:S(2)}) async-start(f32[16,192,128]{2,1,0:T(8,128)} %fusion.17), calls=%async_computation.6 | async-start | bytes 3145728 | tf_op jit(solution)/shard_map/all_to_all | solution.py:175
  205.4 1.1 copy.38
  206.5 0.9 copy_bitcast_fusion
  207.5 29.7 %all-to-all-done.6 = f32[16,192,128]{2,1,0:T(8,128)S(1)} async-done(((f32[16,192,128]{2,1,0:T(8,128)}), f32[16,192,128]{2,1,0:T(8,128)S(1)}, u32[]{:S(2)}, u32[]{:S(2)}) %all-to-all-start.6) | async-done | bytes 1572896 | tf_op jit(solution)/shard_map/all_to_all | solution.py:175
  (54 shorter events, 5.3 us)
Async XLA Ops:
  0.6 38.0 %copy-start = (s32[2048]{0:T(1024)S(1)}, s32[2048]{0:T(1024)}, u32[]{:S(2)}) copy-start(s32[2048]{0:T(1024)} %param.15) | copy-start | bytes 24580
  0.6 55.4 %copy-start.1 = (s32[2048]{0:T(1024)S(1)}, s32[2048]{0:T(1024)}, u32[]{:S(2)}) copy-start(s32[2048]{0:T(1024)} %param.16) | copy-start | bytes 24580
  2.4 17.4 %all-to-all-start.1 = ((bf16[16,64,128]{2,1,0:T(8,128)(2,1)}), bf16[16,64,128]{2,1,0:T(8,128)(2,1)S(1)}, u32[]{:S(2)}, u32[]{:S(2)}) async-start(bf16[16,64,128]{2,1,0:T(8,128)(2,1)} %bitcast.93), calls=%async_computation.1 | async-start | bytes 524288 | tf_op jit(solution)/shard_map/all_to_all | solution.py:64
  19.8 13.5 %all-to-all-start.4 = ((bf16[16,64,128]{2,1,0:T(8,128)(2,1)}), bf16[16,64,128]{2,1,0:T(8,128)(2,1)S(1)}, u32[]{:S(2)}, u32[]{:S(2)}) async-start(bf16[16,64,128]{2,1,0:T(8,128)(2,1)} %bitcast.92), calls=%async_computation.4 | async-start | bytes 524288 | tf_op jit(solution)/shard_map/all_to_all | solution.py:67
  34.5 43.7 %all-to-all-start = ((bf16[16,192,128]{2,1,0:T(8,128)(2,1)}), bf16[16,192,128]{2,1,0:T(8,128)(2,1)S(1)}, u32[]{:S(2)}, u32[]{:S(2)}) async-start(bf16[16,192,128]{2,1,0:T(8,128)(2,1)} %bitcast.2), calls=%async_computation | async-start | bytes 1572864 | tf_op jit(solution)/shard_map/all_to_all | solution.py:75
  56.0 17.5 %copy-start.6 = (bf16[128,512]{1,0:T(8,128)(2,1)S(1)}, bf16[128,512]{1,0:T(8,128)(2,1)}, u32[]{:S(2)}) copy-start(bf16[128,512]{1,0:T(8,128)(2,1)} %param.10) | copy-start | bytes 393220
  56.0 17.5 %copy-start.7 = (bf16[64,512]{1,0:T(8,128)(2,1)S(1)}, bf16[64,512]{1,0:T(8,128)(2,1)}, u32[]{:S(2)}) copy-start(bf16[64,512]{1,0:T(8,128)(2,1)} %param.13) | copy-start | bytes 196612
  56.0 17.6 %copy-start.2 = (s32[1024]{0:T(1024)S(1)}, s32[1024]{0:T(1024)}, u32[]{:S(2)}) copy-start(s32[1024]{0:T(1024)} %param.17) | copy-start | bytes 12292
  79.3 24.7 %all-to-all-start.2 = ((bf16[16,192,128]{2,1,0:T(8,128)(2,1)}), bf16[16,192,128]{2,1,0:T(8,128)(2,1)S(1)}, u32[]{:S(2)}, u32[]{:S(2)}) async-start(bf16[16,192,128]{2,1,0:T(8,128)(2,1)} %bitcast.9), calls=%async_computation.2 | async-start | bytes 1572864 | tf_op jit(solution)/shard_map/all_to_all | solution.py:78
  95.5 4.5 %copy-start.3 = (f32[1024,3072]{0,1:T(8,128)}, f32[1024,3072]{0,1:T(8,128)S(1)}, u32[]{:S(2)}) copy-start(f32[1024,3072]{0,1:T(8,128)S(1)} %get-tuple-element.98) | copy-start | bytes 37748740
  111.2 33.2 %all-to-all-start.3 = ((bf16[16,64,128]{2,1,0:T(8,128)(2,1)}), bf16[16,64,128]{2,1,0:T(8,128)(2,1)S(1)}, u32[]{:S(2)}, u32[]{:S(2)}) async-start(bf16[16,64,128]{2,1,0:T(8,128)(2,1)} %bitcast.11), calls=%async_computation.3 | async-start | bytes 524288 | tf_op jit(solution)/shard_map/all_to_all | solution.py:145
  116.7 18.6 %copy-start.4 = (f32[1024,3072]{0,1:T(8,128)S(1)}, f32[1024,3072]{0,1:T(8,128)}, u32[]{:S(2)}) copy-start(f32[1024,3072]{0,1:T(8,128)} %copy-done.3) | copy-start | bytes 37748740
  144.4 16.1 %all-to-all-start.5 = ((bf16[16,64,128]{2,1,0:T(8,128)(2,1)}), bf16[16,64,128]{2,1,0:T(8,128)(2,1)S(1)}, u32[]{:S(2)}, u32[]{:S(2)}) async-start(bf16[16,64,128]{2,1,0:T(8,128)(2,1)} %bitcast.18), calls=%async_computation.5 | async-start | bytes 524288 | tf_op jit(solution)/shard_map/all_to_all | solution.py:181
  160.5 35.6 %copy-start.5 = (bf16[16,64,128]{2,1,0:T(8,128)(2,1)}, bf16[16,64,128]{2,1,0:T(8,128)(2,1)S(1)}, u32[]{:S(2)}) copy-start(bf16[16,64,128]{2,1,0:T(8,128)(2,1)S(1)} %all-to-all-done.5) | copy-start | bytes 786436
  160.5 35.6 %all-to-all-start.7 = ((f32[16,192,128]{2,1,0:T(8,128)}), f32[16,192,128]{2,1,0:T(8,128)S(1)}, u32[]{:S(2)}, u32[]{:S(2)}) async-start(f32[16,192,128]{2,1,0:T(8,128)} %fusion.18), calls=%async_computation.7 | async-start | bytes 3145728 | tf_op jit(solution)/shard_map/all_to_all | solution.py:176
  196.1 41.1 %all-to-all-start.6 = ((f32[16,192,128]{2,1,0:T(8,128)}), f32[16,192,128]{2,1,0:T(8,128)S(1)}, u32[]{:S(2)}, u32[]{:S(2)}) async-start(f32[16,192,128]{2,1,0:T(8,128)} %fusion.17), calls=%async_computation.6 | async-start | bytes 3145728 | tf_op jit(solution)/shard_map/all_to_all | solution.py:175
where the time goes:
time: 244 us; the launch traced here: 240 us
  waiting for transfers between devices  79.6 us (33%)
  matrix products  56.6 us (23%)
  local copies, waits for them, and re-layouts  54.8 us (22%)
  starting transfers between devices  44.7 us (18%)
  other arithmetic  3.11 us (1%)
    all_to_all x1, waiting for transfers between devices, body(): lax.all_to_all(key_part, 'seq', split_axis=0, concat_axis=0, tiled=True)  29.7 us
    all_to_all x1, waiting for transfers between devices, body(): lax.all_to_all(value_part, 'seq', split_axis=0, concat_axis=0, tiled=True)  26.2 us
    dot_general x1, matrix products, back_step(): jnp.einsum('qd,kd->qk', grad_head, value_blk, preferred_element_type=jnp....  18.6 us
    gather x1, local copies, waits for them, and re-layouts, body(): key_agent = prefix_agent[pre_index]  17.4 us
    gather x1, local copies, waits for them, and re-layouts, body(): key_public = prefix_round[pre_index] < ROUNDS - 2  17.4 us
    dot_general x1, matrix products, block_scores(): jnp.einsum('qd,kd->qk', query_head, key_blk, preferred_element_type=jnp.f...  10.2 us
    all_to_all x1, waiting for transfers between devices, body(): lax.all_to_all(to_head_rows(d_out, devices), 'seq', split_axis=0, concat_...  9.76 us
    dot_general x1, matrix products, back_step(): jnp.dot(grad_scores, key_blk, preferred_element_type=jnp.float32)  9.12 us
  transfers between devices with their start and end apart: 8, of which 6 were waited for; matrix products, arithmetic and copies ran while one was open for 40% of the time, Pallas kernels for 0%

commit v1 on v0

--- a/solution.py
+++ b/solution.py
@@ -1,8 +1,11 @@
+import functools
 import math
 
 import jax
 import jax.numpy as jnp
 from jax import lax
+from jax.experimental import pallas as pl
+from jax.experimental.pallas import tpu as pltpu
 from jax.sharding import PartitionSpec as P
 
 HQ = 16
@@ -198,6 +201,367 @@
     )
 
 
+MESH = pl.DeviceIdType.MESH
+LANES = 4
+BIG = 32768.0
+F32 = jnp.float32
+BF16 = jnp.bfloat16
+
+
+def mm(a, b):
+    return jnp.dot(a, b, preferred_element_type=F32)
+
+
+def plane_kernel(
+    pre, own,
+    pk_ref, pv_ref, q_ref, rk_ref, rv_ref, do_ref, pa_ref, pr_ref, ra_ref,
+    attn_ref, dq_ref, dk_ref, dv_ref,
+    kv_stage, q_stage, kv_buf, q_buf, kext, tri, qt, dot_t, qs, dos,
+    s_buf, p_buf, ds_buf, mx_ref, l_ref, acc_t, kt_buf, vt_buf,
+    att_stage, dq_stage, red_stage, red_buf, own_part, fin_stage,
+    kvz_s, kvz_r, qz_s, qz_r, pg_s, pg_r, red_s, red_r,
+    at_s, at_r, dqs_s, dqs_r, fk_s, fk_r, fv_s, fv_r,
+):
+    keys = pre + own
+    rows = LANES * own
+    span = LANES * keys
+    me = lax.axis_index("seq")
+    z = me // LANES
+    p = me % LANES
+    seq = lambda zz, pp: {"seq": zz * LANES + pp}
+    z_peers = [(z + k) % LANES for k in (2, 3, 1)]
+    pair = p + 1 - 2 * (p % 2)
+    far = (p + 2) % LANES
+    cross = pair + 2 - 4 * (pair // 2)
+    p_peers = [cross, far, pair]
+    scale = DH ** (-0.5)
+    to_two = scale * math.log2(math.e)
+
+    def rcopy(src, dst, ss, rs, zz, pp):
+        return pltpu.make_async_remote_copy(
+            src_ref=src, dst_ref=dst, send_sem=ss, recv_sem=rs,
+            device_id=seq(zz, pp), device_id_type=MESH,
+        )
+
+    barrier = pltpu.get_barrier_semaphore()
+    for o in z_peers:
+        pl.semaphore_signal(barrier, inc=1, device_id=seq(o, p), device_id_type=MESH)
+    for o in p_peers:
+        pl.semaphore_signal(barrier, inc=1, device_id=seq(z, o), device_id_type=MESH)
+
+    for g in range(KVH):
+        cols = slice(g * DH, (g + 1) * DH)
+        kv_stage[g, 0:pre, :] = pk_ref[:, cols]
+        kv_stage[g, pre:keys, :] = rk_ref[:, cols]
+        kv_stage[g, keys:keys + pre, :] = pv_ref[:, cols]
+        kv_stage[g, keys + pre:2 * keys, :] = rv_ref[:, cols]
+        wide = slice(g * 4 * DH, (g + 1) * 4 * DH)
+        q_stage[g, 0:own, :] = q_ref[:, wide]
+        q_stage[g, own:2 * own, :] = do_ref[:, wide]
+    pl.semaphore_wait(barrier, 6)
+
+    def kv_send(o):
+        return rcopy(kv_stage.at[o], kv_buf.at[p, z], kvz_s.at[o], kvz_r.at[z], o, p)
+
+    def kv_recv(o):
+        return rcopy(kv_stage.at[o], kv_buf.at[p, o], kvz_s.at[o], kvz_r.at[o], o, p)
+
+    def q_send(o):
+        return rcopy(q_stage.at[o], q_buf.at[z], qz_s.at[o], qz_r.at[z], o, p)
+
+    def q_recv(o):
+        return rcopy(q_stage.at[o], q_buf.at[o], qz_s.at[o], qz_r.at[o], o, p)
+
+    def pg_send(o, piece):
+        return rcopy(
+            kv_buf.at[p, piece], kv_buf.at[p, piece],
+            pg_s.at[o, piece], pg_r.at[p, piece], z, o,
+        )
+
+    def pg_recv(o, piece):
+        return rcopy(
+            kv_buf.at[o, piece], kv_buf.at[o, piece],
+            pg_s.at[o, piece], pg_r.at[o, piece], z, o,
+        )
+
+    for o in z_peers:
+        kv_send(o).start()
+    kv_buf[p, z] = kv_stage[z]
+    q_buf[z] = q_stage[z]
+    for o in p_peers:
+        pg_send(o, z).start()
+    for o in z_peers:
+        q_send(o).start()
+
+    lane = lax.broadcasted_iota(jnp.int32, (own, DH), 1) - 16
+    sub = lax.broadcasted_iota(jnp.int32, (DH, pre), 0)
+
+    def ext_step(b, carry):
+        at = pl.ds(pl.multiple_of(b * pre, pre), pre)
+        c = b % LANES
+        zz = b // LANES
+        base = zz * keys
+        off = (pr_ref[:, at] >= ROUNDS - 2) & (pa_ref[:, at] != sub) & (sub < 8)
+        kext[c, pl.ds(pl.multiple_of(base, 64), pre), :] = (
+            jnp.where(off, 1.0, 0.0).astype(F32).T.astype(BF16)
+        )
+        late = (lane >= 0) & (lane < b)
+        kext[c, pl.ds(pl.multiple_of(base + pre, 64), own), :] = (
+            jnp.where(late, 1.0, 0.0).astype(F32).astype(BF16)
+        )
+        return carry
+
+    lax.fori_loop(0, LANES * LANES, ext_step, 0)
+    sub_q = lax.broadcasted_iota(jnp.int32, (DH, rows), 0)
+    block_q = (lax.broadcasted_iota(jnp.int32, (DH, rows), 1) // own) * LANES + p
+    ext_q = jnp.where(
+        ((sub_q < 8) & (sub_q == ra_ref[pl.ds(p, 1), :])) | (sub_q - 16 == block_q), -BIG, 0.0
+    ).astype(F32).astype(BF16)
+    for h in range(4):
+        qt[DH:2 * DH, h * rows:(h + 1) * rows] = ext_q
+    row_k = lax.broadcasted_iota(jnp.int32, (span, rows), 0)
+    row_q = lax.broadcasted_iota(jnp.int32, (span, rows), 1)
+    tri[...] = jnp.where(
+        (row_k // keys == row_q // own) & (row_k % keys >= pre)
+        & (row_k % keys - pre > row_q % own),
+        -BIG, 0.0,
+    ).astype(F32)
+    mx_ref[...] = jnp.full(mx_ref.shape, -3.0e38, F32)
+
+    for o in z_peers:
+        kv_recv(o).wait_recv()
+        for d in p_peers:
+            pg_send(d, o).start()
+    for o in z_peers:
+        q_recv(o).wait_recv()
+    for h in range(4):
+        cols = slice(h * DH, (h + 1) * DH)
+        qh = q_buf[:, 0:own, cols].reshape(rows, DH)
+        dh = q_buf[:, own:2 * own, cols].reshape(rows, DH)
+        qs[h * rows:(h + 1) * rows, :] = qh
+        dos[h * rows:(h + 1) * rows, :] = dh
+        qt[0:DH, h * rows:(h + 1) * rows] = qh.T
+        dot_t[:, h * rows:(h + 1) * rows] = dh.T
+
+    def head_at(h):
+        return pl.ds(pl.multiple_of(h * rows, rows), rows)
+
+    def score_chunk(c, diagonal):
+        kc = kv_buf[c, :, 0:keys, :].reshape(span, DH)
+        vc = kv_buf[c, :, keys:2 * keys, :].reshape(span, DH)
+        kt_buf[c] = kc.T
+        vt_buf[c] = vc.T
+
+        def step(h, carry):
+            full = jnp.concatenate(
+                [kv_buf[c, :, 0:keys, :].reshape(span, DH), kext[c]], 1
+            )
+            s = mm(full, qt[:, head_at(h)])
+            if diagonal:
+                s = s + tri[...]
+            s_buf[c, :, head_at(h)] = s
+            mx_ref[:, head_at(h)] = jnp.maximum(
+                mx_ref[:, head_at(h)], jnp.max(s, 0, keepdims=True)
+            )
+            return carry
+
+        lax.fori_loop(0, 4, step, 0)
+
+    score_chunk(p, True)
+    for o in (pair, far, cross):
+        for piece in [z] + z_peers:
+            pg_recv(o, piece).wait_recv()
+        score_chunk(o, False)
+
+    def exp_step(h, carry):
+        at = head_at(h)
+        top = mx_ref[:, at] * to_two
+        total = jnp.zeros((1, rows), F32)
+        acc = jnp.zeros((DH, rows), F32)
+        for c in range(LANES):
+            pu = jnp.exp2(s_buf[c, :, at] * to_two - top)
+            total = total + jnp.sum(pu, 0, keepdims=True)
+            low = pu.astype(BF16)
+            p_buf[c, :, at] = low
+            acc = acc + mm(vt_buf[c], low)
+        inv = 1.0 / total
+        out = (acc * inv).astype(BF16)
+        outf = out.astype(F32)
+        delta = jnp.sum(outf * dot_t[:, at].astype(F32), 0, keepdims=True)
+        mx_ref[:, at] = delta
+        l_ref[:, at] = inv
+        acc_t[:, at] = outf
+        return carry
+
+    lax.fori_loop(0, 4, exp_step, 0)
+    for h in range(4):
+        cols = slice(h * DH, (h + 1) * DH)
+        at = slice(h * rows, (h + 1) * rows)
+        att_stage[:, :, cols] = acc_t[:, at].T.astype(BF16).reshape(LANES, own, DH)
+        dnorm = (dot_t[:, at].astype(F32) * l_ref[:, at]).T
+        dos[at, :] = dnorm.astype(BF16)
+    wide_z = pl.ds(pl.multiple_of(z * 4 * DH, 4 * DH), 4 * DH)
+    one_z = pl.ds(pl.multiple_of(z * DH, DH), DH)
+
+    def at_send(o):
+        return rcopy(att_stage.at[o], attn_ref.at[:, wide_z], at_s.at[o], at_r.at[z], o, p)
+
+    def wide_of(o):
+        return pl.ds(pl.multiple_of(o * 4 * DH, 4 * DH), 4 * DH)
+
+    def one_of(o):
+        return pl.ds(pl.multiple_of(o * DH, DH), DH)
+
+    def at_recv(o):
+        return rcopy(att_stage.at[o], attn_ref.at[:, wide_of(o)], at_s.at[o], at_r.at[o], o, p)
+
+    for o in z_peers:
+        at_send(o).start()
+    attn_ref[:, wide_z] = att_stage[z]
+    acc_t[...] = jnp.zeros(acc_t.shape, F32)
+
+    def back_chunk(c):
+        def step(h, carry):
+            at = head_at(h)
+            vc = kv_buf[c, :, keys:2 * keys, :].reshape(span, DH)
+            dp = mm(vc, dot_t[:, at])
+            pu = p_buf[c, :, at].astype(F32)
+            ds = (pu * ((dp - mx_ref[:, at]) * (l_ref[:, at] * scale))).astype(BF16)
+            ds_buf[:, at] = ds
+            acc_t[:, at] += mm(kt_buf[c], ds)
+            return carry
+
+        lax.fori_loop(0, 4, step, 0)
+        return mm(ds_buf[...], qs[...]), mm(p_buf[c], dos[...])
+
+    def red_send(o):
+        return rcopy(red_stage.at[o], red_buf.at[p], red_s.at[o], red_r.at[p], z, o)
+
+    def red_recv(o):
+        return rcopy(red_stage.at[o], red_buf.at[o], red_s.at[o], red_r.at[o], z, o)
+
+    for o in p_peers:
+        dkc, dvc = back_chunk(o)
+        red_stage[o, :, 0:keys, :] = dkc.astype(BF16).reshape(LANES, keys, DH)
+        red_stage[o, :, keys:2 * keys, :] = dvc.astype(BF16).reshape(LANES, keys, DH)
+        red_send(o).start()
+    dkc, dvc = back_chunk(p)
+    own_part[:, 0:keys, :] = dkc.reshape(LANES, keys, DH)
+    own_part[:, keys:2 * keys, :] = dvc.reshape(LANES, keys, DH)
+    for h in range(4):
+        cols = slice(h * DH, (h + 1) * DH)
+        at = slice(h * rows, (h + 1) * rows)
+        dq_stage[:, :, cols] = acc_t[:, at].T.astype(BF16).reshape(LANES, own, DH)
+
+    def dq_send(o):
+        return rcopy(dq_stage.at[o], dq_ref.at[:, wide_z], dqs_s.at[o], dqs_r.at[z], o, p)
+
+    def dq_recv(o):
+        return rcopy(dq_stage.at[o], dq_ref.at[:, wide_of(o)], dqs_s.at[o], dqs_r.at[o], o, p)
+
+    for o in z_peers:
+        dq_send(o).start()
+    dq_ref[:, wide_z] = dq_stage[z]
+
+    for o in (pair, cross, far):
+        red_recv(o).wait_recv()
+    total = own_part[...]
+    for o in p_peers:
+        total = total + red_buf[o].astype(F32)
+    fin_stage[...] = total.astype(BF16)
+
+    def fk(o, at, r):
+        return rcopy(fin_stage.at[o, pl.ds(0, keys)], dk_ref.at[:, at], fk_s.at[o], fk_r.at[r], o, p)
+
+    def fv(o, at, r):
+        return rcopy(
+            fin_stage.at[o, pl.ds(keys, keys)], dv_ref.at[:, at], fv_s.at[o], fv_r.at[r], o, p
+        )
+
+    for o in z_peers:
+        fk(o, one_z, z).start()
+        fv(o, one_z, z).start()
+    dk_ref[:, one_z] = fin_stage[z, 0:keys, :]
+    dv_ref[:, one_z] = fin_stage[z, keys:2 * keys, :]
+
+    for o in z_peers:
+        at_recv(o).wait_recv()
+        dq_recv(o).wait_recv()
+        fk(o, one_of(o), o).wait_recv()
+        fv(o, one_of(o), o).wait_recv()
+    for o in z_peers:
+        kv_send(o).wait_send()
+        q_send(o).wait_send()
+        at_send(o).wait_send()
+        dq_send(o).wait_send()
+        fk(o, one_z, z).wait_send()
+        fv(o, one_z, z).wait_send()
+    for o in p_peers:
+        for piece in [z] + z_peers:
+            pg_send(o, piece).wait_send()
+        red_send(o).wait_send()
+
+
+def plane_body(
+    prefix_keys, prefix_values, round_queries, round_keys, round_values, d_out,
+    prefix_agent, prefix_round, round_agent,
+):
+    pre, own = prefix_keys.shape[0], round_keys.shape[0]
+    keys, rows = pre + own, LANES * own
+    span, wide = LANES * keys, 4 * rows
+    agents = round_agent.reshape(LANES, LANES, own).transpose(1, 0, 2).reshape(LANES, rows)
+    vmem = pl.BlockSpec(memory_space=pltpu.VMEM)
+    dma = pltpu.SemaphoreType.DMA
+    attn, dq, dk, dv = pl.pallas_call(
+        functools.partial(plane_kernel, pre, own),
+        out_shape=(
+            jax.ShapeDtypeStruct(round_queries.shape, BF16),
+            jax.ShapeDtypeStruct(round_queries.shape, BF16),
+            jax.ShapeDtypeStruct((keys, KVH * DH), BF16),
+            jax.ShapeDtypeStruct((keys, KVH * DH), BF16),
+        ),
+        in_specs=[vmem] * 9,
+        out_specs=(vmem,) * 4,
+        scratch_shapes=[
+            pltpu.VMEM((LANES, 2 * keys, DH), BF16),
+            pltpu.VMEM((LANES, 2 * own, 4 * DH), BF16),
+            pltpu.VMEM((LANES, LANES, 2 * keys, DH), BF16),
+            pltpu.VMEM((LANES, 2 * own, 4 * DH), BF16),
+            pltpu.VMEM((LANES, span, DH), BF16),
+            pltpu.VMEM((span, rows), F32),
+            pltpu.VMEM((2 * DH, wide), BF16),
+            pltpu.VMEM((DH, wide), BF16),
+            pltpu.VMEM((wide, DH), BF16),
+            pltpu.VMEM((wide, DH), BF16),
+            pltpu.VMEM((LANES, span, wide), F32),
+            pltpu.VMEM((LANES, span, wide), BF16),
+            pltpu.VMEM((span, wide), BF16),
+            pltpu.VMEM((1, wide), F32),
+            pltpu.VMEM((1, wide), F32),
+            pltpu.VMEM((DH, wide), F32),
+            pltpu.VMEM((LANES, DH, span), BF16),
+            pltpu.VMEM((LANES, DH, span), BF16),
+            pltpu.VMEM((LANES, own, 4 * DH), BF16),
+            pltpu.VMEM((LANES, own, 4 * DH), BF16),
+            pltpu.VMEM((LANES, LANES, 2 * keys, DH), BF16),
+            pltpu.VMEM((LANES, LANES, 2 * keys, DH), BF16),
+            pltpu.VMEM((LANES, 2 * keys, DH), F32),
+            pltpu.VMEM((LANES, 2 * keys, DH), BF16),
+            dma((LANES,)), dma((LANES,)), dma((LANES,)), dma((LANES,)),
+            dma((LANES, LANES)), dma((LANES, LANES)), dma((LANES,)), dma((LANES,)),
+            dma((LANES,)), dma((LANES,)), dma((LANES,)), dma((LANES,)),
+            dma((LANES,)), dma((LANES,)), dma((LANES,)), dma((LANES,)),
+        ],
+        compiler_params=pltpu.CompilerParams(
+            collective_id=0, has_side_effects=True, vmem_limit_bytes=56 * 1024 * 1024
+        ),
+    )(
+        prefix_keys, prefix_values, round_queries, round_keys, round_values, d_out,
+        prefix_agent.reshape(1, -1), prefix_round.reshape(1, -1), agents,
+    )
+    return attn, dq, dk[pre:], dv[pre:], dk[:pre], dv[:pre]
+
+
 def solution(mesh):
     placed = (
         P(("group", "seq"), None),
@@ -210,8 +574,9 @@
         P("group"),
         P("group"),
     )
+    planes = mesh.shape["seq"] == KVH * LANES
     return jax.shard_map(
-        body,
+        plane_body if planes else body,
         mesh=mesh,
         in_specs=placed,
         out_specs=(

time: 244 us -> 73.7 us (0.30); the launches traced: 240 us -> 73.5 us
  waiting for transfers between devices: 79.6 us -> 0 us
  Pallas kernels: 0 us -> 65.2 us
  matrix products: 56.6 us -> 0 us
  local copies, waits for them, and re-layouts: 54.8 us -> 7.62 us
  starting transfers between devices: 44.7 us -> 0 us
  other arithmetic: 3.11 us -> 0 us
    all_to_all x8 -> x0, waiting for transfers between devices: 79.6 us -> none  [the longest x1 29.7 us: body(): lax.all_to_all(key_part, 'seq', split_axis=0, concat_axis=0, tiled=True)]
    pallas_call x0 -> x1, Pallas kernels: none -> 65.2 us  [plane_body(): pl.pallas_call(functools.partial(plane_kernel, pre, own), out_shape=(jax....]
    dot_general x6 -> x0, matrix products: 56.6 us -> none  [the longest x1 18.6 us: back_step(): jnp.einsum('qd,kd->qk', grad_head, value_blk, preferred_element_type=jnp....]
    all_to_all x8 -> x0, starting transfers between devices: 44.7 us -> none  [the longest x1 9.08 us: body(): lax.all_to_all(key_part, 'seq', split_axis=0, concat_axis=0, tiled=True)]
    gather x3 -> x0, local copies, waits for them, and re-layouts: 39.3 us -> none  [the longest x1 17.4 us: body(): key_agent = prefix_agent[pre_index]]
    unnamed x20 -> x8, local copies, waits for them, and re-layouts: 8.05 us -> 1.75 us
    slice x5 -> x4, local copies, waits for them, and re-layouts: 0.95 us -> 4.42 us  [plane_body(): return (attn, dq, dk[pre:], dv[pre:], dk[:pre], dv[:pre])]
  transfers between devices with their start and end apart: 8 -> 0, of which waited for: 6 -> 0; matrix products, arithmetic and copies ran while one was open for 40% -> 0% of each run, Pallas kernels for 0% -> 0%
where the time goes in v1:
time: 73.7 us; the launch traced here: 73.5 us
  Pallas kernels  65.2 us (88%)
  local copies, waits for them, and re-layouts  7.62 us (10%)
    pallas_call x1, Pallas kernels, plane_body(): pl.pallas_call(functools.partial(plane_kernel, pre, own), out_shape=(jax....  65.2 us
    slice x4, local copies, waits for them, and re-layouts, plane_body(): return (attn, dq, dk[pre:], dv[pre:], dk[:pre], dv[:pre])  4.42 us
    unnamed x8, local copies, waits for them, and re-layouts  1.75 us

profile of v1, /device:TPU:0, one launch (start us, length us, event | category | flops | bytes accessed | tf_op | source)
XLA Modules:
  0.0 73.5 jit_solution(17640059090146255243)
XLA Ops:
  0.6 0.8 %reshape.26 = s32[4,4,64]{2,1,0:T(4,128)S(1)} reshape(s32[1024]{0:T(1024)} %param.17) | data formatting | bytes 8192 | tf_op jit(solution)/shard_map/reshape | solution.py:512
  1.4 0.7 reshape.27.ra_ref
  2.1 65.2 %shard_map.136 = (bf16[64,2048]{1,0:T(8,128)(2,1)}, bf16[64,2048]{1,0:T(8,128)(2,1)}, bf16[192,512]{1,0:T(8,128)(2,1)}, bf16[192,512]{1,0:T(8,128)(2,1)}) custom-call(bf16[128,512]{1,0:T(8,128)(2,1)} %pk_ref.1, bf16[128,512]{1,0:T(8,128)(2,1)} %pv_ref.1, bf16[64,2048]{1,0:T(8,128)(2,1)} %q_ref.1, bf16[64,512]{1,0:T(8,128)(2,1)} %rk_ref.1, ...), custom_call_target="tpu_custom_call" | custom-call | tf_op jit(solution)/shard_map/pallas_call | solution.py:515
  67.3 0.0 copy-start.2
  67.3 1.5 %slice.12 = bf16[64,512]{1,0:T(8,128)(2,1)} slice(bf16[192,512]{1,0:T(8,128)(2,1)} %get-tuple-element.12), slice={[128:192], [0:512]} | slice | bytes 131072 | tf_op jit(solution)/shard_map/slice | solution.py:562
  68.8 0.0 copy-start.1
  68.8 1.6 %slice.14 = bf16[128,512]{1,0:T(8,128)(2,1)} slice(bf16[192,512]{1,0:T(8,128)(2,1)} %get-tuple-element.12), slice={[0:128], [0:512]} | slice | bytes 262144 | tf_op jit(solution)/shard_map/slice | solution.py:562
  70.4 0.0 copy-done.2
  70.4 0.6 slice.13
  71.1 0.7 slice.15
  71.7 0.0 copy-done.1
  71.7 0.0 copy-start
  71.7 0.7 copy.18
  72.4 0.3 copy-done
  72.8 0.7 copy.19
  (1 shorter events, 0.0 us)
Async XLA Ops:
  67.3 3.1 %copy-start.2 = (bf16[192,512]{1,0:T(8,128)(2,1)S(1)}, bf16[192,512]{1,0:T(8,128)(2,1)}, u32[]{:S(2)}) copy-start(bf16[192,512]{1,0:T(8,128)(2,1)} %get-tuple-element.13) | copy-start | bytes 589828
  68.8 2.9 %copy-start.1 = (bf16[64,2048]{1,0:T(8,128)(2,1)S(1)}, bf16[64,2048]{1,0:T(8,128)(2,1)}, u32[]{:S(2)}) copy-start(bf16[64,2048]{1,0:T(8,128)(2,1)} %get-tuple-element.20) | copy-start | bytes 786436
  71.7 1.0 %copy-start = (bf16[64,2048]{1,0:T(8,128)(2,1)S(1)}, bf16[64,2048]{1,0:T(8,128)(2,1)}, u32[]{:S(2)}) copy-start(bf16[64,2048]{1,0:T(8,128)(2,1)} %get-tuple-element.21) | copy-start | bytes 786436

commit v2 on v1

--- a/solution.py
+++ b/solution.py
@@ -220,7 +220,7 @@
     s_buf, p_buf, ds_buf, mx_ref, l_ref, acc_t, kt_buf, vt_buf,
     att_stage, dq_stage, red_stage, red_buf, own_part, fin_stage,
     kvz_s, kvz_r, qz_s, qz_r, pg_s, pg_r, red_s, red_r,
-    at_s, at_r, dqs_s, dqs_r, fk_s, fk_r, fv_s, fv_r,
+    at_s, at_r, dqs_s, dqs_r, fin_s, fin_r,
 ):
     keys = pre + own
     rows = LANES * own
@@ -260,38 +260,49 @@
         q_stage[g, own:2 * own, :] = do_ref[:, wide]
     pl.semaphore_wait(barrier, 6)
 
-    def kv_send(o):
-        return rcopy(kv_stage.at[o], kv_buf.at[p, z], kvz_s.at[o], kvz_r.at[z], o, p)
-
-    def kv_recv(o):
-        return rcopy(kv_stage.at[o], kv_buf.at[p, o], kvz_s.at[o], kvz_r.at[o], o, p)
-
-    def q_send(o):
-        return rcopy(q_stage.at[o], q_buf.at[z], qz_s.at[o], qz_r.at[z], o, p)
-
-    def q_recv(o):
-        return rcopy(q_stage.at[o], q_buf.at[o], qz_s.at[o], qz_r.at[o], o, p)
-
-    def pg_send(o, piece):
+    def half(i, n):
+        return pl.ds(i * n, n)
+
+    def kv_copy(i, o, at, slot):
         return rcopy(
-            kv_buf.at[p, piece], kv_buf.at[p, piece],
-            pg_s.at[o, piece], pg_r.at[p, piece], z, o,
-        )
-
-    def pg_recv(o, piece):
+            kv_stage.at[o, half(i, keys)], kv_buf.at[p, at, half(i, keys)],
+            kvz_s.at[i, o], kvz_r.at[i, slot], o, p,
+        )
+
+    def q_copy(i, o, slot):
         return rcopy(
-            kv_buf.at[o, piece], kv_buf.at[o, piece],
-            pg_s.at[o, piece], pg_r.at[o, piece], z, o,
-        )
-
-    for o in z_peers:
-        kv_send(o).start()
+            q_stage.at[o, half(i, own)], q_buf.at[slot, half(i, own)],
+            qz_s.at[i, o], qz_r.at[i, slot], o, p,
+        )
+
+    def pg_copy(i, chunk, piece, o, slot):
+        return rcopy(
+            kv_buf.at[chunk, piece, half(i, keys)], kv_buf.at[chunk, piece, half(i, keys)],
+            pg_s.at[i, slot, piece], pg_r.at[i, chunk, piece], z, o,
+        )
+
+    pieces = [z] + z_peers
+
+    def pg_mine(i, piece):
+        pg_copy(i, p, piece, far, 0).start()
+        pg_copy(i, p, piece, pair, 1).start()
+
+    def pg_pass(i, piece):
+        pg_copy(i, far, piece, pair, 2).wait_recv()
+        pg_copy(i, far, piece, pair, 2).start()
+
+    def pg_wait(i, chunk):
+        for piece in pieces:
+            pg_copy(i, chunk, piece, pair, 2).wait_recv()
+
+    for i in range(2):
+        for o in z_peers:
+            kv_copy(i, o, z, z).start()
+        for o in z_peers:
+            q_copy(i, o, z).start()
     kv_buf[p, z] = kv_stage[z]
     q_buf[z] = q_stage[z]
-    for o in p_peers:
-        pg_send(o, z).start()
-    for o in z_peers:
-        q_send(o).start()
+    pg_mine(0, z)
 
     lane = lax.broadcasted_iota(jnp.int32, (own, DH), 1) - 16
     sub = lax.broadcasted_iota(jnp.int32, (DH, pre), 0)
@@ -328,29 +339,27 @@
     ).astype(F32)
     mx_ref[...] = jnp.full(mx_ref.shape, -3.0e38, F32)
 
-    for o in z_peers:
-        kv_recv(o).wait_recv()
-        for d in p_peers:
-            pg_send(d, o).start()
-    for o in z_peers:
-        q_recv(o).wait_recv()
+    for n in range(LANES):
+        if n > 0:
+            kv_copy(0, pieces[n], pieces[n], pieces[n]).wait_recv()
+            pg_mine(0, pieces[n])
+            pg_pass(0, pieces[n - 1])
+    pg_pass(0, pieces[3])
+    pg_mine(1, z)
+    for o in z_peers:
+        q_copy(0, o, o).wait_recv()
     for h in range(4):
         cols = slice(h * DH, (h + 1) * DH)
         qh = q_buf[:, 0:own, cols].reshape(rows, DH)
-        dh = q_buf[:, own:2 * own, cols].reshape(rows, DH)
         qs[h * rows:(h + 1) * rows, :] = qh
-        dos[h * rows:(h + 1) * rows, :] = dh
         qt[0:DH, h * rows:(h + 1) * rows] = qh.T
-        dot_t[:, h * rows:(h + 1) * rows] = dh.T
 
     def head_at(h):
         return pl.ds(pl.multiple_of(h * rows, rows), rows)
 
     def score_chunk(c, diagonal):
         kc = kv_buf[c, :, 0:keys, :].reshape(span, DH)
-        vc = kv_buf[c, :, keys:2 * keys, :].reshape(span, DH)
         kt_buf[c] = kc.T
-        vt_buf[c] = vc.T
 
         def step(h, carry):
             full = jnp.concatenate(
@@ -367,11 +376,26 @@
 
         lax.fori_loop(0, 4, step, 0)
 
+    def turn_values(c):
+        vt_buf[c] = kv_buf[c, :, keys:2 * keys, :].reshape(span, DH).T
+
     score_chunk(p, True)
-    for o in (pair, far, cross):
-        for piece in [z] + z_peers:
-            pg_recv(o, piece).wait_recv()
-        score_chunk(o, False)
+    pg_wait(0, pair)
+    score_chunk(pair, False)
+    for o in z_peers:
+        kv_copy(1, o, o, o).wait_recv()
+        pg_mine(1, o)
+    turn_values(p)
+    score_chunk(far, False)
+    pg_wait(0, cross)
+    for piece in pieces:
+        pg_pass(1, piece)
+    score_chunk(cross, False)
+    turn_values(far)
+    pg_wait(1, pair)
+    turn_values(pair)
+    pg_wait(1, cross)
+    turn_values(cross)
 
     def exp_step(h, carry):
         at = head_at(h)
@@ -385,12 +409,8 @@
             p_buf[c, :, at] = low
             acc = acc + mm(vt_buf[c], low)
         inv = 1.0 / total
-        out = (acc * inv).astype(BF16)
-        outf = out.astype(F32)
-        delta = jnp.sum(outf * dot_t[:, at].astype(F32), 0, keepdims=True)
-        mx_ref[:, at] = delta
         l_ref[:, at] = inv
-        acc_t[:, at] = outf
+        acc_t[:, at] = (acc * inv).astype(BF16).astype(F32)
         return carry
 
     lax.fori_loop(0, 4, exp_step, 0)
@@ -398,8 +418,6 @@
         cols = slice(h * DH, (h + 1) * DH)
         at = slice(h * rows, (h + 1) * rows)
         att_stage[:, :, cols] = acc_t[:, at].T.astype(BF16).reshape(LANES, own, DH)
-        dnorm = (dot_t[:, at].astype(F32) * l_ref[:, at]).T
-        dos[at, :] = dnorm.astype(BF16)
     wide_z = pl.ds(pl.multiple_of(z * 4 * DH, 4 * DH), 4 * DH)
     one_z = pl.ds(pl.multiple_of(z * DH, DH), DH)
 
@@ -418,36 +436,72 @@
     for o in z_peers:
         at_send(o).start()
     attn_ref[:, wide_z] = att_stage[z]
+    for o in z_peers:
+        q_copy(1, o, o).wait_recv()
+    for h in range(4):
+        cols = slice(h * DH, (h + 1) * DH)
+        at = slice(h * rows, (h + 1) * rows)
+        dh = q_buf[:, own:2 * own, cols].reshape(rows, DH).astype(F32).T
+        dot_t[:, at] = dh.astype(BF16)
+        mx_ref[:, at] = jnp.sum(acc_t[:, at] * dh, 0, keepdims=True)
+        dos[at, :] = (dh * l_ref[:, at]).T.astype(BF16)
     acc_t[...] = jnp.zeros(acc_t.shape, F32)
 
-    def back_chunk(c):
+    def red_copy(i, slot):
+        return rcopy(
+            red_stage.at[i, slot], red_buf.at[i, slot],
+            red_s.at[i, slot], red_r.at[i, slot], z, far if slot == 1 else pair,
+        )
+
+    def reduce_sends(i, left, right):
+        def part(c):
+            return mm(left[c], right[...]).reshape(LANES, keys, DH)
+
+        red_stage[i, 0] = part(cross).astype(BF16)
+        red_copy(i, 0).start()
+        red_stage[i, 2] = part(pair).astype(BF16)
+        red_copy(i, 2).start()
+        ours = part(far)
+        red_copy(i, 0).wait_recv()
+        red_stage[i, 1] = (ours + red_buf[i, 0].astype(F32)).astype(BF16)
+        red_copy(i, 1).start()
+        own_part[i] = part(p)
+
+    def fin_copy(i, o, at, slot):
+        return rcopy(
+            fin_stage.at[i, o], (dk_ref, dv_ref)[i].at[:, at],
+            fin_s.at[i, o], fin_r.at[i, slot], o, p,
+        )
+
+    def finish(i):
+        red_copy(i, 2).wait_recv()
+        red_copy(i, 1).wait_recv()
+        fin_stage[i] = (
+            own_part[i] + red_buf[i, 1].astype(F32) + red_buf[i, 2].astype(F32)
+        ).astype(BF16)
+        for o in z_peers:
+            fin_copy(i, o, one_z, z).start()
+        (dk_ref, dv_ref)[i][:, one_z] = fin_stage[i, z]
+
+    def grad_chunk(c):
         def step(h, carry):
             at = head_at(h)
             vc = kv_buf[c, :, keys:2 * keys, :].reshape(span, DH)
             dp = mm(vc, dot_t[:, at])
             pu = p_buf[c, :, at].astype(F32)
             ds = (pu * ((dp - mx_ref[:, at]) * (l_ref[:, at] * scale))).astype(BF16)
-            ds_buf[:, at] = ds
+            ds_buf[c, :, at] = ds
             acc_t[:, at] += mm(kt_buf[c], ds)
             return carry
 
         lax.fori_loop(0, 4, step, 0)
-        return mm(ds_buf[...], qs[...]), mm(p_buf[c], dos[...])
-
-    def red_send(o):
-        return rcopy(red_stage.at[o], red_buf.at[p], red_s.at[o], red_r.at[p], z, o)
-
-    def red_recv(o):
-        return rcopy(red_stage.at[o], red_buf.at[o], red_s.at[o], red_r.at[o], z, o)
-
-    for o in p_peers:
-        dkc, dvc = back_chunk(o)
-        red_stage[o, :, 0:keys, :] = dkc.astype(BF16).reshape(LANES, keys, DH)
-        red_stage[o, :, keys:2 * keys, :] = dvc.astype(BF16).reshape(LANES, keys, DH)
-        red_send(o).start()
-    dkc, dvc = back_chunk(p)
-    own_part[:, 0:keys, :] = dkc.reshape(LANES, keys, DH)
-    own_part[:, keys:2 * keys, :] = dvc.reshape(LANES, keys, DH)
+
+    reduce_sends(1, p_buf, dos)
+    grad_chunk(cross)
+    grad_chunk(far)
+    finish(1)
+    grad_chunk(pair)
+    grad_chunk(p)
     for h in range(4):
         cols = slice(h * DH, (h + 1) * DH)
         at = slice(h * rows, (h + 1) * rows)
@@ -463,43 +517,42 @@
         dq_send(o).start()
     dq_ref[:, wide_z] = dq_stage[z]
 
-    for o in (pair, cross, far):
-        red_recv(o).wait_recv()
-    total = own_part[...]
-    for o in p_peers:
-        total = total + red_buf[o].astype(F32)
-    fin_stage[...] = total.astype(BF16)
-
-    def fk(o, at, r):
-        return rcopy(fin_stage.at[o, pl.ds(0, keys)], dk_ref.at[:, at], fk_s.at[o], fk_r.at[r], o, p)
-
-    def fv(o, at, r):
-        return rcopy(
-            fin_stage.at[o, pl.ds(keys, keys)], dv_ref.at[:, at], fv_s.at[o], fv_r.at[r], o, p
-        )
-
-    for o in z_peers:
-        fk(o, one_z, z).start()
-        fv(o, one_z, z).start()
-    dk_ref[:, one_z] = fin_stage[z, 0:keys, :]
-    dv_ref[:, one_z] = fin_stage[z, keys:2 * keys, :]
+    reduce_sends(0, ds_buf, qs)
+    finish(0)
 
     for o in z_peers:
         at_recv(o).wait_recv()
         dq_recv(o).wait_recv()
-        fk(o, one_of(o), o).wait_recv()
-        fv(o, one_of(o), o).wait_recv()
-    for o in z_peers:
-        kv_send(o).wait_send()
-        q_send(o).wait_send()
+        fin_copy(0, o, one_of(o), o).wait_recv()
+        fin_copy(1, o, one_of(o), o).wait_recv()
+    for o in z_peers:
         at_send(o).wait_send()
         dq_send(o).wait_send()
-        fk(o, one_z, z).wait_send()
-        fv(o, one_z, z).wait_send()
-    for o in p_peers:
-        for piece in [z] + z_peers:
-            pg_send(o, piece).wait_send()
-        red_send(o).wait_send()
+        for i in range(2):
+            kv_copy(i, o, z, z).wait_send()
+            q_copy(i, o, z).wait_send()
+            fin_copy(i, o, one_z, z).wait_send()
+    for i in range(2):
+        for slot in range(3):
+            red_copy(i, slot).wait_send()
+        for piece in pieces:
+            pg_copy(i, p, piece, far, 0).wait_send()
+            pg_copy(i, p, piece, pair, 1).wait_send()
+            pg_copy(i, far, piece, pair, 2).wait_send()
+
+
+def place_kernel(pre, attn, dq, dk, dv, o_attn, o_dq, o_rk, o_rv, o_pk, o_pv, sems):
+    own = dk.shape[0] - pre
+    moves = [
+        (attn, o_attn), (dq, o_dq),
+        (dk.at[pl.ds(pre, own)], o_rk), (dv.at[pl.ds(pre, own)], o_rv),
+        (dk.at[pl.ds(0, pre)], o_pk), (dv.at[pl.ds(0, pre)], o_pv),
+    ]
+    copies = [pltpu.make_async_copy(a, b, sems.at[n]) for n, (a, b) in enumerate(moves)]
+    for copy in copies:
+        copy.start()
+    for copy in copies:
+        copy.wait()
 
 
 def plane_body(
@@ -535,7 +588,7 @@
             pltpu.VMEM((wide, DH), BF16),
             pltpu.VMEM((LANES, span, wide), F32),
             pltpu.VMEM((LANES, span, wide), BF16),
-            pltpu.VMEM((span, wide), BF16),
+            pltpu.VMEM((LANES, span, wide), BF16),
             pltpu.VMEM((1, wide), F32),
             pltpu.VMEM((1, wide), F32),
             pltpu.VMEM((DH, wide), F32),
@@ -543,14 +596,14 @@
             pltpu.VMEM((LANES, DH, span), BF16),
             pltpu.VMEM((LANES, own, 4 * DH), BF16),
             pltpu.VMEM((LANES, own, 4 * DH), BF16),
-            pltpu.VMEM((LANES, LANES, 2 * keys, DH), BF16),
-            pltpu.VMEM((LANES, LANES, 2 * keys, DH), BF16),
-            pltpu.VMEM((LANES, 2 * keys, DH), F32),
-            pltpu.VMEM((LANES, 2 * keys, DH), BF16),
+            pltpu.VMEM((2, 3, LANES, keys, DH), BF16),
+            pltpu.VMEM((2, 3, LANES, keys, DH), BF16),
+            pltpu.VMEM((2, LANES, keys, DH), F32),
+            pltpu.VMEM((2, LANES, keys, DH), BF16),
+            dma((2, LANES)), dma((2, LANES)), dma((2, LANES)), dma((2, LANES)),
+            dma((2, 3, LANES)), dma((2, LANES, LANES)), dma((2, 3)), dma((2, 3)),
             dma((LANES,)), dma((LANES,)), dma((LANES,)), dma((LANES,)),
-            dma((LANES, LANES)), dma((LANES, LANES)), dma((LANES,)), dma((LANES,)),
-            dma((LANES,)), dma((LANES,)), dma((LANES,)), dma((LANES,)),
-            dma((LANES,)), dma((LANES,)), dma((LANES,)), dma((LANES,)),
+            dma((2, LANES)), dma((2, LANES)),
         ],
         compiler_params=pltpu.CompilerParams(
             collective_id=0, has_side_effects=True, vmem_limit_bytes=56 * 1024 * 1024
@@ -559,7 +612,18 @@
         prefix_keys, prefix_values, round_queries, round_keys, round_values, d_out,
         prefix_agent.reshape(1, -1), prefix_round.reshape(1, -1), agents,
     )
-    return attn, dq, dk[pre:], dv[pre:], dk[:pre], dv[:pre]
+    free = pl.BlockSpec(memory_space=pl.ANY)
+    low = lambda a: jax.ShapeDtypeStruct(a.shape, BF16)
+    return pl.pallas_call(
+        functools.partial(place_kernel, pre),
+        out_shape=(
+            low(round_queries), low(round_queries), low(round_keys), low(round_keys),
+            low(prefix_keys), low(prefix_keys),
+        ),
+        in_specs=[vmem] * 4,
+        out_specs=(free,) * 6,
+        scratch_shapes=[dma((6,))],
+    )(attn, dq, dk, dv)
 
 
 def solution(mesh):

time: 73.7 us -> 67.6 us (0.917)
  local copies, waits for them, and re-layouts: 7.62 us -> 1.45 us
    slice x4 -> x0, local copies, waits for them, and re-layouts: 4.42 us -> none  [plane_body(): return (attn, dq, dk[pre:], dv[pre:], dk[:pre], dv[:pre])]
    pallas_call x0 -> x1, Pallas kernels: none -> 2.11 us  [plane_body(): pl.pallas_call(functools.partial(place_kernel, pre), out_shape=(low(round...]
    pallas_call x1, Pallas kernels: 65.2 us -> 63.2 us  [plane_body(): pl.pallas_call(functools.partial(plane_kernel, pre, own), out_shape=(jax....]
    unnamed x8 -> x0, local copies, waits for them, and re-layouts: 1.75 us -> none
where the time goes in v2:
time: 67.6 us; the launch traced here: 67.4 us
  Pallas kernels  65.4 us (97%)
  local copies, waits for them, and re-layouts  1.45 us (2%)
    pallas_call x1, Pallas kernels, plane_body(): pl.pallas_call(functools.partial(plane_kernel, pre, own), out_shape=(jax....  63.2 us
    pallas_call x1, Pallas kernels, plane_body(): pl.pallas_call(functools.partial(place_kernel, pre), out_shape=(low(round...  2.11 us
    reshape x2, local copies, waits for them, and re-layouts, plane_body(): round_agent.reshape(LANES, LANES, own).transpose(1, 0, 2)  1.44 us

profile of v2, /device:TPU:0, one launch (start us, length us, event | category | flops | bytes accessed | tf_op | source)
XLA Modules:
  0.0 67.4 jit_solution(14445682111529213736)
XLA Ops:
  0.6 0.8 %reshape.26 = s32[4,4,64]{2,1,0:T(4,128)S(1)} reshape(s32[1024]{0:T(1024)} %param.17) | data formatting | bytes 8192 | tf_op jit(solution)/shard_map/reshape | solution.py:565
  1.4 0.7 %reshape.27.ra_ref = s32[4,256]{1,0:T(4,128)} reshape(s32[4,4,64]{2,1,0:T(4,128)S(1)} %copy.15) | data formatting | bytes 8192 | tf_op jit(solution)/shard_map/reshape | solution.py:565
  2.1 63.2 %shard_map.136 = (bf16[64,2048]{1,0:T(8,128)(2,1)}, bf16[64,2048]{1,0:T(8,128)(2,1)}, bf16[192,512]{1,0:T(8,128)(2,1)}, bf16[192,512]{1,0:T(8,128)(2,1)}) custom-call(bf16[128,512]{1,0:T(8,128)(2,1)} %pk_ref.1, bf16[128,512]{1,0:T(8,128)(2,1)} %pv_ref.1, bf16[64,2048]{1,0:T(8,128)(2,1)} %q_ref.1, bf16[64,512]{1,0:T(8,128)(2,1)} %rk_ref.1, ...), custom_call_target="tpu_custom_call" | custom-call | tf_op jit(solution)/shard_map/pallas_call | solution.py:568
  65.3 2.1 %shard_map.137 = (bf16[64,2048]{1,0:T(8,128)(2,1)}, bf16[64,2048]{1,0:T(8,128)(2,1)}, bf16[64,512]{1,0:T(8,128)(2,1)}, bf16[64,512]{1,0:T(8,128)(2,1)}, bf16[128...) custom-call(bf16[64,2048]{1,0:T(8,128)(2,1)} %get-tuple-element.10.attn, bf16[64,2048]{1,0:T(8,128)(2,1)} %get-tuple-element.11.dq, ...), custom_call_target="tpu_custom_call" | custom-call | tf_op jit(solution)/shard_map/pallas_call | solution.py:617
  (1 shorter events, 0.0 us)
